TPU v7x, 32 devices: a whole 2x2x4 slice. The times are simulated.
32 devices in a mesh: xb: 4 (over z), yb: 8 (over y, x, core).
Axes of the slice: x: 2, y: 2, z: 4, core: 2. Of those that a mesh axis runs over, the one named last changes fastest.
Arguments:
- tracers: float32 [2, 16, 192, 512], P(None, None, 'yb', 'xb'), may hold values from -6 to 6
- velocities: float32 [2, 16, 192, 512], P(None, None, 'yb', 'xb'), may hold values from -0.24 to 0.24
- level_counts: int32 [192, 512], P('yb', 'xb'), may hold values from 0 to 16, as said below
- lateral_diffusivity: float32 [192, 512], P('yb', 'xb'), may hold values from 0.02 to 0.2
- vertical_diffusivity: float32 [192, 512], P('yb', 'xb'), may hold values from 0.1 to 10
- forcing: float32 [192, 512], P('yb', 'xb'), may hold values from -125 to 125
Outputs:
- tracers_new: bfloat16 [2, 16, 192, 512], P(None, None, 'yb', 'xb')
- surface_height: float32 [192, 512], P('yb', 'xb')
Inputs may be any that keep to these rules, and one draw needn't show every extreme that they name: level_counts is 0 exactly on land columns, and land is the union of 8 rectangles, each 64 to 128 columns wide (periodic in x) and 24 to 64 rows high; every other column has 1 or more wet levels.
All inputs are finite; a program needn't handle non-finite values.
Results may differ from a plain program's by a relative error of at most 0.001.
Values sent between devices are 32-bit elements; how exact they have to be, the bound alone decides.
A program may use at most 64 MiB of HBM per device.

v0:
```python
import functools

import jax
import jax.numpy as jnp
from jax import lax
from jax.experimental import pallas as pl
from jax.experimental.pallas import tpu as pltpu
from jax.sharding import PartitionSpec as P

ITERS = 3
MESH = pl.DeviceIdType.MESH
SHIFT = 4.1
SCALE = 4.0
DIRECT = 64
NORTH, SOUTH = 0, 1
LEFT, RIGHT = 0, 1


def add_up(terms):
    while len(terms) > 1:
        terms = [sum(terms[i:i + 2][1:], terms[i]) for i in range(0, len(terms), 2)]
    return terms[0]


def inner(a, b, moments):
    return add_up([x * y * moments[i + j] for i, x in enumerate(a) for j, y in enumerate(b)])


def cg_coefficients(moments):
    one = jnp.ones_like(moments[0])
    zero = jnp.zeros_like(one)
    height = [zero] * ITERS
    residual = [one]
    direction = [one]
    norm = moments[0]
    for step in range(ITERS):
        image = [SHIFT * d for d in direction] + [zero]
        for i, d in enumerate(direction):
            image[i + 1] = image[i + 1] + SCALE * d
        alpha = jnp.clip(norm / inner(direction, image, moments), 0.0, 10.0)
        for i, d in enumerate(direction):
            height[i] = height[i] + alpha * d
        if step + 1 < ITERS:
            padded = residual + [zero]
            residual = [p - alpha * m for p, m in zip(padded, image)]
            new = jnp.maximum(inner(residual, residual, moments), 0.0)
            beta = new / norm
            longer = direction + [zero]
            direction = [p + beta * d for p, d in zip(residual, longer)]
            norm = new
    return height


def kernel(
    nx, ny, levels,
    trac, vel, counts_in, lateral_in, vertical_in, forcing_in,
    rounded, out_height,
    c_ext, f_ext, strip_e, strip_w, counts_i, kv, force,
    y_send, y_recv, x_recv, corner_recv, col_recv,
    rhs, r2_x, r2_corner, r2_y, parts,
    values, ratios, inverses, wide_coefs, flat_coefs,
    load_sem, send1, recv1, send2, recv2, send_r, recv_r, ready,
):
    h, lanes = rhs.shape
    ext = h + 8
    mx, my = lax.axis_index("xb"), lax.axis_index("yb")
    east, west = lax.rem(mx + 1, nx), lax.rem(mx + nx - 1, nx)
    north, south = lax.rem(my + 1, ny), lax.rem(my + ny - 1, ny)

    direct = nx * ny <= DIRECT
    me = my * nx + mx

    barrier = pltpu.get_barrier_semaphore()
    near = [(north, mx), (south, mx)]
    far = [(lax.rem(my + d, ny), mx) for d in range(2, ny - 1)]
    peers = near + [(my, lax.rem(mx + d, nx)) for d in range(1, nx)] + far
    loads = [
        pltpu.make_async_copy(trac, c_ext.at[:, :, pl.ds(0, h), :], load_sem.at[0]),
        pltpu.make_async_copy(vel, f_ext.at[:, :, pl.ds(0, h), :], load_sem.at[1]),
        pltpu.make_async_copy(counts_in, counts_i, load_sem.at[2]),
        pltpu.make_async_copy(lateral_in, strip_e.at[2], load_sem.at[3]),
        pltpu.make_async_copy(lateral_in, strip_w.at[2], load_sem.at[4]),
        pltpu.make_async_copy(vertical_in, kv, load_sem.at[5]),
        pltpu.make_async_copy(forcing_in, force, load_sem.at[6]),
    ]
    for load in loads:
        load.start()
    for y, x in peers:
        pl.semaphore_signal(barrier, inc=1, device_id={"xb": x, "yb": y}, device_id_type=MESH)
    for load in loads:
        load.wait()

    lane = lax.broadcasted_iota(jnp.int32, (h, lanes), 1)
    counts_here = counts_i[...].astype(jnp.float32)
    strip_e[1] = counts_here
    strip_w[1] = counts_here

    for n, ref in enumerate((c_ext, f_ext)):
        for t in range(2):
            rows = pl.ds((2 * n + t) * levels, levels)
            y_send[NORTH, rows] = ref[t, :, 0:2, :]
            y_send[SOUTH, rows] = ref[t, :, h - 2:h, :]

    pack_e = jnp.zeros((h, lanes), jnp.float32)
    pack_w = jnp.zeros((h, lanes), jnp.float32)
    pair = lane // 2
    for p in range(4 * levels):
        ref = c_ext if p < 2 * levels else f_ext
        plane = ref[(p // levels) % 2, p % levels, 0:h, :]
        turned = pltpu.roll(plane, (2 * p + 2) % lanes, 1)
        pack_e = jnp.where(pair == p, turned, pack_e)
        pack_w = jnp.where(pair == (p + 1) % (lanes // 2), turned, pack_w)
    pack_w = pltpu.roll(pack_w, lanes - 2, 1)
    strip_e[0] = pack_e
    strip_w[0] = pack_w

    pl.semaphore_wait(barrier, len(peers))

    def remote(src, dst, send, recv, i, y, x):
        return pltpu.make_async_remote_copy(
            src_ref=src, dst_ref=dst, send_sem=send.at[i], recv_sem=recv.at[i],
            device_id={"xb": x, "yb": y}, device_id_type=MESH,
        )

    low, high = pl.ds(0, 8), pl.ds(h - 8, 8)
    cols = pl.ds(1, 2)
    first = [
        remote(strip_e.at[:, high], corner_recv.at[LEFT, SOUTH], send1, recv1, 0, north, east),
        remote(strip_e.at[:, low], corner_recv.at[LEFT, NORTH], send1, recv1, 1, south, east),
        remote(strip_w.at[:, high], corner_recv.at[RIGHT, SOUTH], send1, recv1, 2, north, west),
        remote(strip_w.at[:, low], corner_recv.at[RIGHT, NORTH], send1, recv1, 3, south, west),
        remote(strip_e, x_recv.at[LEFT], send1, recv1, 4, my, east),
        remote(strip_w, x_recv.at[RIGHT], send1, recv1, 5, my, west),
        remote(strip_e.at[cols, high], col_recv.at[SOUTH], send1, recv1, 6, north, mx),
        remote(strip_e.at[cols, low], col_recv.at[NORTH], send1, recv1, 7, south, mx),
        remote(y_send.at[SOUTH], y_recv.at[SOUTH], send1, recv1, 8, north, mx),
        remote(y_send.at[NORTH], y_recv.at[NORTH], send1, recv1, 9, south, mx),
    ]
    for y, x in near:
        pl.semaphore_signal(ready.at[0], inc=1, device_id={"xb": x, "yb": y}, device_id_type=MESH)
    for copy in first[4:]:
        copy.start()
    if direct:
        for y, x in far:
            pl.semaphore_signal(ready.at[1], inc=1, device_id={"xb": x, "yb": y}, device_id_type=MESH)
    pl.semaphore_wait(ready.at[0], len(near))
    for copy in first[:4]:
        copy.start()
    coef = kv[...]
    zero = jnp.zeros_like(coef)
    previous_link = zero
    previous_ratio = zero
    for k in range(levels):
        link = jnp.where(k + 1.0 < counts_here, coef, 0.0) if k + 1 < levels else zero
        inverse = 1.0 / (1.0 + previous_link + link - previous_link * previous_ratio)
        previous_ratio = link * inverse
        previous_link = link
        inverses[k] = inverse
        ratios[k] = previous_ratio
    for copy in first:
        copy.wait()

    half = lax.broadcasted_iota(jnp.int32, (8, lanes), 0) < 4
    row = lax.broadcasted_iota(jnp.int32, (ext, lanes), 0)
    lane = lax.broadcasted_iota(jnp.int32, (ext, lanes), 1)
    beyond = ((row >= h) & (row < h + 4) & (my == ny - 1)) | ((row >= h + 4) & (my == 0))

    def tall(main, from_north, from_south):
        return jnp.concatenate([main, jnp.where(half, from_north, from_south)], axis=0)

    for n, ref in enumerate((c_ext, f_ext)):
        for t in range(2):
            rows = pl.ds((2 * n + t) * levels, levels)
            ref[t, :, h:h + 2, :] = y_recv[NORTH, rows]
            ref[t, :, h + 2:h + 6, :] = jnp.zeros((levels, 4, lanes), jnp.float32)
            ref[t, :, h + 6:h + 8, :] = y_recv[SOUTH, rows]

    def tall_field(i):
        main = tall(strip_e[i], col_recv[NORTH, i - 1], col_recv[SOUTH, i - 1])
        left = tall(x_recv[LEFT, i], corner_recv[LEFT, NORTH, i], corner_recv[LEFT, SOUTH, i])
        right = tall(x_recv[RIGHT, i], corner_recv[RIGHT, NORTH, i], corner_recv[RIGHT, SOUTH, i])
        return main, left, right

    def up(x):
        return pltpu.roll(x, x.shape[0] - 1, 0)

    def down(x):
        return pltpu.roll(x, 1, 0)

    n_main, n_left, n_right = [jnp.where(beyond, 0.0, x) for x in tall_field(1)]
    h_main, h_left, h_right = tall_field(2)

    first_lane = lane == 0
    last_lane = lane == lanes - 1

    def eastward(x, right):
        return jnp.where(last_lane, pltpu.roll(right, lanes - 1, 1), pltpu.roll(x, lanes - 1, 1))

    def westward(x, left):
        return jnp.where(first_lane, pltpu.roll(left, 1, 1), pltpu.roll(x, 1, 1))

    odd = lane % 2 == 1
    blank = jnp.zeros((8, lanes), jnp.float32)
    own_e = jnp.concatenate([strip_e[0], blank], axis=0)
    own_w = jnp.concatenate([strip_w[0], blank], axis=0)
    left = tall(x_recv[LEFT, 0], corner_recv[LEFT, NORTH, 0], corner_recv[LEFT, SOUTH, 0])
    right = tall(x_recv[RIGHT, 0], corner_recv[RIGHT, NORTH, 0], corner_recv[RIGHT, SOUTH, 0])

    def lroll(x, shift):
        return pltpu.roll(x, shift % lanes, 1)

    s_c = jnp.where(odd, left, right)
    s_w = jnp.where(odd, lroll(left, 1), lroll(own_e, -1))
    s_e = jnp.where(odd, lroll(own_w, 1), lroll(right, -1))
    lower = lane < 2 * levels

    def spread(x, n):
        start = 2 * levels * (2 + n)
        return jnp.where(lower, lroll(x, -start), lroll(x, 2 * levels - start))

    s_ue, s_uw, s_v = spread(s_c, 0), spread(s_w, 0), spread(s_c, 1)
    n_c = jnp.where(odd, n_left[:, lanes - 1:], n_right[:, :1])
    n_w = jnp.where(odd, n_left[:, lanes - 2:lanes - 1], n_main[:, lanes - 1:])
    n_e = jnp.where(odd, n_main[:, :1], n_right[:, 1:2])
    rank = ((lane // 2) % levels).astype(jnp.float32)
    s_ue_open = jnp.where(rank < jnp.minimum(n_c, n_e), s_ue, 0.0)
    s_uw_open = jnp.where(rank < jnp.minimum(n_w, n_c), s_uw, 0.0)
    s_v_open = jnp.where(rank < jnp.minimum(n_c, up(n_c)), s_v, 0.0)
    flux_e = jnp.maximum(s_ue_open, 0.0) * s_c + jnp.minimum(s_ue_open, 0.0) * s_e
    flux_w = jnp.maximum(s_uw_open, 0.0) * s_w + jnp.minimum(s_uw_open, 0.0) * s_c
    flux_n = jnp.maximum(s_v_open, 0.0) * s_c + jnp.minimum(s_v_open, 0.0) * up(s_c)
    s_adv = jnp.where(rank < n_c, s_c - (flux_e - flux_w + flux_n - down(flux_n)), 0.0)

    face_e = jnp.minimum(n_main, eastward(n_main, n_right))
    face_w = jnp.minimum(n_main, westward(n_main, n_left))
    face_n = jnp.minimum(n_main, up(n_main))
    face_s = down(face_n)
    mix_e = (0.5 * (h_main + eastward(h_main, h_right)))[:h]
    mix_w = (0.5 * (h_main + westward(h_main, h_left)))[:h]
    mix_n = 0.5 * (h_main + up(h_main))
    mix_s = down(mix_n)[:h]
    mix_n = mix_n[:h]

    def transport(c, edge_c, edge_a, wide, flat):
        stay, ue_neg, uw_pos, vn_neg, vs_pos = wide
        keep, ce, cw, cn, cs = flat
        c_east = jnp.where(last_lane, edge_c, lroll(c, -1))
        c_west = jnp.where(first_lane, edge_c, lroll(c, 1))
        adv = stay * c - ue_neg * c_east + uw_pos * c_west - vn_neg * up(c) + vs_pos * down(c)
        mid = adv[:h]
        a_east = jnp.where(last_lane[:h], edge_a[:h], lroll(mid, -1))
        a_west = jnp.where(first_lane[:h], edge_a[:h], lroll(mid, 1))
        return keep * mid + ce * a_east + cw * a_west + cn * up(adv)[:h] + cs * down(adv)[:h]

    d_c = lroll(s_c, -2 * levels) - s_c
    d_adv = lroll(s_adv, -2 * levels) - s_adv
    previous_link = zero
    previous = zero
    for k in range(levels):
        u = f_ext[0, k]
        v = f_ext[1, k]
        u_west = jnp.where(first_lane, lroll(s_ue, -(2 * k + 1)), lroll(u, 1))
        ue = jnp.where(k < face_e, u, 0.0)
        uw = jnp.where(k < face_w, u_west, 0.0)
        vn = jnp.where(k < face_n, v, 0.0)
        ue_neg = jnp.minimum(ue, 0.0)
        uw_pos = jnp.maximum(uw, 0.0)
        vn_neg = jnp.minimum(vn, 0.0)
        vs = down(vn)
        vs_pos = jnp.maximum(vs, 0.0)
        out = (ue - ue_neg) - (uw - uw_pos) + (vn - vn_neg) - (vs - vs_pos)
        stay = jnp.where(k < n_main, 1.0 - out, 0.0)
        ce = jnp.where(k < face_e[:h], mix_e, 0.0)
        cw = jnp.where(k < face_w[:h], mix_w, 0.0)
        cn = jnp.where(k < face_n[:h], mix_n, 0.0)
        cs = jnp.where(k < face_s[:h], mix_s, 0.0)
        keep = 1.0 - ((ce + cw) + (cn + cs))
        wide = (stay, ue_neg, uw_pos, vn_neg, vs_pos)
        flat = (keep, ce, cw, cn, cs)
        for i in range(5):
            wide_coefs[k, i] = wide[i]
            flat_coefs[k, i] = flat[i]
        c = c_ext[1, k] - c_ext[0, k]
        mixed = transport(c, lroll(d_c, -(2 * k + 1)), lroll(d_adv, -(2 * k + 1)), wide, flat)
        previous = (mixed + previous_link * previous) * inverses[k]
        values[0, k] = previous
        previous_link = jnp.where(k + 1.0 < counts_here, coef, 0.0)

    result = previous
    column_sum = result
    for k in range(levels - 2, -1, -1):
        result = values[0, k] + ratios[k] * result
        column_sum = column_sum + result
    rhs_here = force[...] + column_sum / levels
    rhs[...] = rhs_here

    second = [
        remote(rhs.at[high], r2_corner.at[LEFT, SOUTH], send2, recv2, 0, north, east),
        remote(rhs.at[low], r2_corner.at[LEFT, NORTH], send2, recv2, 1, south, east),
        remote(rhs.at[high], r2_corner.at[RIGHT, SOUTH], send2, recv2, 2, north, west),
        remote(rhs.at[low], r2_corner.at[RIGHT, NORTH], send2, recv2, 3, south, west),
        remote(rhs, r2_x.at[LEFT], send2, recv2, 4, my, east),
        remote(rhs, r2_x.at[RIGHT], send2, recv2, 5, my, west),
        remote(rhs.at[high], r2_y.at[SOUTH], send2, recv2, 6, north, mx),
        remote(rhs.at[low], r2_y.at[NORTH], send2, recv2, 7, south, mx),
    ]
    for copy in second:
        copy.start()

    previous_link = zero
    previous = [zero, zero]
    for k in range(levels):
        wide = [wide_coefs[k, i] for i in range(5)]
        flat = [flat_coefs[k, i] for i in range(5)]
        inverse = inverses[k]
        for t in range(2):
            turn = -(2 * (t * levels + k) + 1)
            mixed = transport(c_ext[t, k], lroll(s_c, turn), lroll(s_adv, turn), wide, flat)
            previous[t] = (mixed + previous_link * previous[t]) * inverse
            values[t, k] = previous[t]
        previous_link = jnp.where(k + 1.0 < counts_here, coef, 0.0)
    for t in range(2):
        result = previous[t]
        rounded[t, levels - 1] = result.astype(jnp.bfloat16)
        for k in range(levels - 2, -1, -1):
            result = values[t, k] + ratios[k] * result
            rounded[t, k] = result.astype(jnp.bfloat16)

    lefty = lane >= lanes // 2

    def side(left_field, right_field):
        return jnp.where(lefty, left_field, right_field)

    def wide_east(x, y):
        a, b = lroll(x, -1), lroll(y, -1)
        return jnp.where(last_lane, b, a), jnp.where(last_lane, a, b)

    def wide_west(x, y):
        a, b = lroll(x, 1), lroll(y, 1)
        return jnp.where(first_lane, b, a), jnp.where(first_lane, a, b)

    scale = 1.0 / (levels * SCALE)
    deep = (n_main * scale, side(n_left, n_right) * scale)
    deep_e = [jnp.minimum(a, b) for a, b in zip(deep, wide_east(*deep))]
    deep_w = wide_west(*deep_e)
    deep_n = [jnp.minimum(a, up(a)) for a in deep]
    deep_s = [down(a) for a in deep_n]
    centre = [
        (0.1 - SHIFT) / SCALE + ((a + b) + (c + d)) for a, b, c, d in zip(deep_e, deep_w, deep_n, deep_s)
    ]

    def apply(field):
        at_e, at_w = wide_east(*field), wide_west(*field)
        return tuple(
            centre[i] * field[i] - deep_e[i] * at_e[i] - deep_w[i] * at_w[i]
            - deep_n[i] * up(field[i]) - deep_s[i] * down(field[i])
            for i in range(2)
        )

    for copy in second:
        copy.wait()
    r_left = tall(r2_x[LEFT], r2_corner[LEFT, NORTH], r2_corner[LEFT, SOUTH])
    r_right = tall(r2_x[RIGHT], r2_corner[RIGHT, NORTH], r2_corner[RIGHT, SOUTH])
    v0 = (tall(rhs_here, r2_y[NORTH], r2_y[SOUTH]), side(r_left, r_right))
    v1 = apply(v0)
    v2 = apply(v1)
    v3 = apply(v2)
    basis = [x[0][:h] for x in (v0, v1, v2, v3)]

    def partial(i, j):
        return jnp.sum(basis[i] * basis[j], axis=0, keepdims=True)

    rows = [partial(m // 2, m - m // 2) for m in range(2 * ITERS)]
    rows.append(jnp.zeros((8 - len(rows), lanes), jnp.float32))
    part = jnp.concatenate(rows, axis=0)
    place = lax.broadcasted_iota(jnp.int32, (8, lanes), 1)
    part = jnp.sum(part, axis=1, keepdims=True)
    part = jnp.where(place == lax.broadcasted_iota(jnp.int32, (8, lanes), 0), part, 0.0)
    part = jnp.sum(part, axis=0, keepdims=True)
    if direct:
        parts[me] = part
        pl.semaphore_wait(ready.at[1], len(far))
        copies = []
        for dy in range(ny):
            for dx in range(nx):
                if dx or dy:
                    y, x = lax.rem(my + dy, ny), lax.rem(mx + dx, nx)
                    copies.append(remote(parts.at[me], parts.at[me], send_r, recv_r, dy * nx + dx, y, x))
        for copy in copies:
            copy.start()
        for copy in copies:
            copy.wait()
        total = add_up([parts[i] for i in range(nx * ny)])
    else:
        parts[mx] = part
        copies = []
        for d in range(1, nx):
            copies.append(remote(parts.at[mx], parts.at[mx], send_r, recv_r, d, my, lax.rem(mx + d, nx)))
        for copy in copies:
            copy.start()
        for copy in copies:
            copy.wait()
        mine = nx + my
        parts[mine] = add_up([parts[i] for i in range(nx)])
        copies = []
        for d in range(1, ny):
            copies.append(remote(parts.at[mine], parts.at[mine], send_r, recv_r, nx + d, lax.rem(my + d, ny), mx))
        for copy in copies:
            copy.start()
        for copy in copies:
            copy.wait()
        total = add_up([parts[nx + i] for i in range(ny)])
    moments = [
        jnp.sum(jnp.where(place[:1] == m, total, 0.0), axis=1, keepdims=True) for m in range(2 * ITERS)
    ]
    weights = cg_coefficients(moments)
    out_height[...] = sum(w * b for w, b in zip(weights, basis))


def write_out(rounded, height, out_tracers, out_height, sem):
    copies = [
        pltpu.make_async_copy(rounded, out_tracers, sem.at[0]),
        pltpu.make_async_copy(height, out_height, sem.at[1]),
    ]
    for copy in copies:
        copy.start()
    for copy in copies:
        copy.wait()


def local(tracers, velocities, level_counts, lateral_diffusivity, vertical_diffusivity, forcing):
    levels = tracers.shape[1]
    h, lanes = forcing.shape
    assert tracers.shape[0] == 2 and 8 * levels == lanes and h % 8 == 0
    nx, ny = lax.axis_size("xb"), lax.axis_size("yb")
    f32 = jnp.float32
    ext = h + 8
    slots = nx * ny if nx * ny <= DIRECT else nx + ny
    dma = pltpu.SemaphoreType.DMA
    vmem = pltpu.VMEM
    held = pl.pallas_call(
        functools.partial(kernel, nx, ny, levels),
        out_shape=(vmem(tracers.shape, jnp.bfloat16), vmem(forcing.shape, f32)),
        in_specs=[pl.BlockSpec(memory_space=pl.ANY)] * 6,
        out_specs=(pl.BlockSpec(memory_space=vmem),) * 2,
        scratch_shapes=[
            vmem((2, levels, ext, lanes), f32),
            vmem((2, levels, ext, lanes), f32),
            vmem((3, h, lanes), f32),
            vmem((3, h, lanes), f32),
            vmem((h, lanes), jnp.int32),
            vmem((h, lanes), f32),
            vmem((h, lanes), f32),
            vmem((2, 4 * levels, 2, lanes), f32),
            vmem((2, 4 * levels, 2, lanes), f32),
            vmem((2, 3, h, lanes), f32),
            vmem((2, 2, 3, 8, lanes), f32),
            vmem((2, 2, 8, lanes), f32),
            vmem((h, lanes), f32),
            vmem((2, h, lanes), f32),
            vmem((2, 2, 8, lanes), f32),
            vmem((2, 8, lanes), f32),
            vmem((slots, 1, lanes), f32),
            vmem((2, levels, h, lanes), f32),
            vmem((levels, h, lanes), f32),
            vmem((levels, h, lanes), f32),
            vmem((levels, 5, ext, lanes), f32),
            vmem((levels, 5, h, lanes), f32),
            dma((7,)),
            dma((10,)), dma((10,)),
            dma((8,)), dma((8,)),
            dma((slots,)), dma((slots,)),
            pltpu.SemaphoreType.REGULAR((2,)),
        ],
        compiler_params=pltpu.CompilerParams(collective_id=0, has_side_effects=True),
        name="ocean_step",
    )(tracers, velocities, level_counts, lateral_diffusivity, vertical_diffusivity, forcing)
    return pl.pallas_call(
        write_out,
        out_shape=(
            jax.ShapeDtypeStruct(tracers.shape, jnp.bfloat16),
            jax.ShapeDtypeStruct(forcing.shape, f32),
        ),
        in_specs=[pl.BlockSpec(memory_space=vmem)] * 2,
        out_specs=(pl.BlockSpec(memory_space=pl.ANY),) * 2,
        scratch_shapes=[dma((2,))],
        name="write_out",
    )(*[pltpu.with_memory_space_constraint(x, vmem) for x in held])


def solution(mesh):
    return jax.shard_map(
        local,
        mesh=mesh,
        in_specs=(
            P(None, None, "yb", "xb"),
            P(None, None, "yb", "xb"),
            P("yb", "xb"),
            P("yb", "xb"),
            P("yb", "xb"),
            P("yb", "xb"),
        ),
        out_specs=(P(None, None, "yb", "xb"), P("yb", "xb")),
        check_vma=False,
    )
```

profile of v0, /device:TPU:0, one launch (start us, length us, event | category | flops | bytes accessed | tf_op | source)
XLA Modules:
  0.0 23.9 jit_solution(13589472782626607686)
XLA Ops:
  0.6 22.5 %ocean_step.1 = (bf16[2,16,24,128]{3,2,1,0:T(8,128)(2,1)S(1)}, f32[24,128]{1,0:T(8,128)S(1)}) custom-call(f32[2,16,24,128]{3,2,1,0:T(8,128)} %trac.1, f32[2,16,24,128]{3,2,1,0:T(8,128)} %vel.1, s32[24,128]{1,0:T(8,128)} %counts_in.1, f32[24,128]{1,0:T(8,128)} %lateral_in.1, f32[24,128]{1,0:T(8,128)} %vertical_in.1, f32[24,128]{1,0:T(8,128)} %forcing_in.1), custom_call_target="tpu_custom_call" | custom-call | tf_op jit(solution)/shard_map/ocean_step/pallas_call | solution.py:441
  23.2 0.7 %write_out.1 = (bf16[2,16,24,128]{3,2,1,0:T(8,128)(2,1)}, f32[24,128]{1,0:T(8,128)}) custom-call(bf16[2,16,24,128]{3,2,1,0:T(8,128)(2,1)S(1)} %get-tuple-element.4.rounded, f32[24,128]{1,0:T(8,128)S(1)} %get-tuple-element.5.height), custom_call_target="tpu_custom_call" | custom-call | tf_op jit(solution)/shard_map/write_out/pallas_call | solution.py:478
where the time goes:
time: 24 us; the launch traced here: 23.9 us
  Pallas kernels  23.2 us (97%)
  between operations  0.64 us (3%)
    pallas_call x1, Pallas kernels, local(): pl.pallas_call(functools.partial(kernel, nx, ny, levels), out_shape=(vmem...  22.5 us
    pallas_call x1, Pallas kernels, local(): pl.pallas_call(write_out, out_shape=(jax.ShapeDtypeStruct(tracers.shape,...  0.7 us

commit v1 on v0

v1 whole, which is shorter than its diff:
```python
import functools

import jax
import jax.numpy as jnp
from jax import lax
from jax.experimental import pallas as pl
from jax.experimental.pallas import tpu as pltpu
from jax.sharding import PartitionSpec as P

ITERS = 3
MESH = pl.DeviceIdType.MESH
SHIFT = 4.1
SCALE = 4.0
DIRECT = 64
NORTH, SOUTH = 0, 1
LEFT, RIGHT = 0, 1
TEMP, DIFF, EASTWARD, NORTHWARD = range(4)


def add_up(terms):
    while len(terms) > 1:
        terms = [sum(terms[i:i + 2][1:], terms[i]) for i in range(0, len(terms), 2)]
    return terms[0]


def inner(a, b, moments):
    return add_up([x * y * moments[i + j] for i, x in enumerate(a) for j, y in enumerate(b)])


def cg_coefficients(moments):
    one = jnp.ones_like(moments[0])
    zero = jnp.zeros_like(one)
    height = [zero] * ITERS
    residual = [one]
    direction = [one]
    norm = moments[0]
    for step in range(ITERS):
        image = [SHIFT * d for d in direction] + [zero]
        for i, d in enumerate(direction):
            image[i + 1] = image[i + 1] + SCALE * d
        alpha = jnp.clip(norm / inner(direction, image, moments), 0.0, 10.0)
        for i, d in enumerate(direction):
            height[i] = height[i] + alpha * d
        if step + 1 < ITERS:
            padded = residual + [zero]
            residual = [p - alpha * m for p, m in zip(padded, image)]
            new = jnp.maximum(inner(residual, residual, moments), 0.0)
            beta = new / norm
            longer = direction + [zero]
            direction = [p + beta * d for p, d in zip(residual, longer)]
            norm = new
    return height


def kernel(
    nx, ny, levels,
    trac, vel, counts_in, lateral_in, vertical_in, forcing_in,
    rounded, out_height,
    wide, salt, counts_i, lateral, kv, force,
    strips, corners, y_send, x_recv, corner_recv, y_recv,
    advected, values, ratios, inverses, parts,
    load_sem, send1, recv1, send_r, recv_r, ready,
):
    h, lanes = force.shape
    ext = h + 8
    slots = lanes // levels
    mx, my = lax.axis_index("xb"), lax.axis_index("yb")
    east, west = lax.rem(mx + 1, nx), lax.rem(mx + nx - 1, nx)
    north, south = lax.rem(my + 1, ny), lax.rem(my + ny - 1, ny)

    direct = nx * ny <= DIRECT
    me = my * nx + mx

    barrier = pltpu.get_barrier_semaphore()
    near = [(north, mx), (south, mx)]
    far = [(lax.rem(my + d, ny), mx) for d in range(2, ny - 1)]
    peers = near + [(my, lax.rem(mx + d, nx)) for d in range(1, nx)] + far
    own = pl.ds(0, h)
    loads = [
        pltpu.make_async_copy(trac.at[0], wide.at[TEMP, :, own, :], load_sem.at[0]),
        pltpu.make_async_copy(trac.at[1], salt, load_sem.at[1]),
        pltpu.make_async_copy(vel, wide.at[pl.ds(EASTWARD, 2), :, own, :], load_sem.at[2]),
        pltpu.make_async_copy(counts_in, counts_i, load_sem.at[3]),
        pltpu.make_async_copy(lateral_in, lateral, load_sem.at[4]),
        pltpu.make_async_copy(vertical_in, kv, load_sem.at[5]),
        pltpu.make_async_copy(forcing_in, force, load_sem.at[6]),
    ]
    for load in loads:
        load.start()
    for y, x in peers:
        pl.semaphore_signal(barrier, inc=1, device_id={"xb": x, "yb": y}, device_id_type=MESH)
    for load in loads:
        load.wait()

    def lroll(x, shift):
        return pltpu.roll(x, shift % lanes, 1)

    def up(x):
        return pltpu.roll(x, x.shape[0] - 1, 0)

    def down(x):
        return pltpu.roll(x, 1, 0)

    def turn(x):
        return pltpu.roll(x, 4, 0)

    def spread(x):
        shift = slots
        while shift < lanes:
            x = x + lroll(x, shift)
            shift *= 2
        return x

    half = lax.broadcasted_iota(jnp.int32, (8, lanes), 0) < 4
    fourth = lax.broadcasted_iota(jnp.int32, (8, lanes), 0) == 3
    lane = lax.broadcasted_iota(jnp.int32, (h, lanes), 1)
    slot = lane % slots
    group = lane // slots
    gap = (slot < 2) | (slot >= 6)
    n_own = counts_i[...].astype(jnp.float32)
    h_own = lateral[...]
    f_own = force[...]
    face_e = jnp.minimum(n_own, lroll(n_own, -1))
    face_low = jnp.minimum(n_own[:8], up(n_own[:8]))

    def low_pair(a, b):
        return jnp.where(half, a[:8], turn(b[:8]))

    def high_pair(a, b):
        return jnp.where(half, turn(b[h - 8:]), a[h - 8:])

    pack = [jnp.zeros((h, lanes), jnp.float32)] * 4
    for k in range(levels):
        t = wide[TEMP, k, 0:h, :]
        u = wide[EASTWARD, k, 0:h, :]
        v = wide[NORTHWARD, k, 0:h, :]
        d = salt[k] - t
        wide[DIFF, k, 0:h, :] = d
        flux = jnp.maximum(u, 0.0) * d + jnp.minimum(u, 0.0) * lroll(d, -1)
        u_out = jnp.where(lane == 3, jnp.where(k < face_e, flux, 0.0), u)
        here = group == k
        for i, x in enumerate((t, d, u_out, v)):
            pack[i] = jnp.where(here, lroll(x, slots * k + 4), pack[i])
        flux = jnp.maximum(v[:8], 0.0) * d[:8] + jnp.minimum(v[:8], 0.0) * up(d[:8])
        v_low = jnp.where(fourth, jnp.where(k < face_low, flux, 0.0), v[:8])
        y_send[NORTH, k] = low_pair(d, u)
        y_send[NORTH, levels + k] = low_pair(v_low, t)
        y_send[SOUTH, k] = high_pair(d, u)
        y_send[SOUTH, levels + k] = high_pair(v, t)
    t_own, d_own, u_edge, v_edge = pack
    for i, x in enumerate((n_own, h_own, f_own)):
        a, b = slots * i, slots * (i + 3)
        t_own = jnp.where((group == i) & gap, lroll(x, a + 4), t_own)
        t_own = jnp.where((group == i + 3) & (slot < 2), lroll(x, b + 2), t_own)
        t_own = jnp.where((group == i + 3) & (slot >= 6), lroll(x, b + 6), t_own)
    n_edge = spread(jnp.where(lane < slots, lroll(n_own, 4), 0.0))
    h_edge = spread(jnp.where(lane < slots, lroll(h_own, 4), 0.0))
    western = slot < 4
    sent = [
        [jnp.where(western, d_own, lroll(u_edge, 4)), jnp.where(western, v_edge, lroll(t_own, 4))],
        [jnp.where(western, lroll(u_edge, -4), d_own), jnp.where(western, lroll(t_own, -4), v_edge)],
    ]
    for i, (a, b) in enumerate(sent):
        strips[i, 0] = a
        strips[i, 1] = b
        corners[i, NORTH] = low_pair(a, b)
        corners[i, SOUTH] = high_pair(a, b)
    extra = [(n_own, h_own), (f_own, t_own), (d_own, u_edge), (n_edge, h_edge)]
    for i, (a, b) in enumerate(extra):
        y_send[NORTH, 2 * levels + i] = low_pair(a, b)
        y_send[SOUTH, 2 * levels + i] = high_pair(a, b)

    pl.semaphore_wait(barrier, len(peers))

    def remote(src, dst, send, recv, i, y, x):
        return pltpu.make_async_remote_copy(
            src_ref=src, dst_ref=dst, send_sem=send.at[i], recv_sem=recv.at[i],
            device_id={"xb": x, "yb": y}, device_id_type=MESH,
        )

    for y, x in near:
        pl.semaphore_signal(ready.at[0], inc=1, device_id={"xb": x, "yb": y}, device_id_type=MESH)
    straight = [
        remote(strips.at[0], x_recv.at[LEFT], send1, recv1, 4, my, east),
        remote(strips.at[1], x_recv.at[RIGHT], send1, recv1, 5, my, west),
        remote(y_send.at[SOUTH], y_recv.at[SOUTH], send1, recv1, 6, north, mx),
        remote(y_send.at[NORTH], y_recv.at[NORTH], send1, recv1, 7, south, mx),
    ]
    diagonal = [
        remote(corners.at[0, SOUTH], corner_recv.at[LEFT, SOUTH], send1, recv1, 0, north, east),
        remote(corners.at[0, NORTH], corner_recv.at[LEFT, NORTH], send1, recv1, 1, south, east),
        remote(corners.at[1, SOUTH], corner_recv.at[RIGHT, SOUTH], send1, recv1, 2, north, west),
        remote(corners.at[1, NORTH], corner_recv.at[RIGHT, NORTH], send1, recv1, 3, south, west),
    ]
    for copy in straight:
        copy.start()
    if direct:
        for y, x in far:
            pl.semaphore_signal(ready.at[1], inc=1, device_id={"xb": x, "yb": y}, device_id_type=MESH)
    pl.semaphore_wait(ready.at[0], len(near))
    for copy in diagonal:
        copy.start()

    coef = kv[...]
    zero = jnp.zeros_like(coef)
    previous_link = zero
    previous_ratio = zero
    for k in range(levels):
        link = jnp.where(k + 1.0 < n_own, coef, 0.0) if k + 1 < levels else zero
        inverse = 1.0 / (1.0 + previous_link + link - previous_link * previous_ratio)
        previous_ratio = link * inverse
        previous_link = link
        inverses[k] = inverse
        ratios[k] = previous_ratio

    for copy in straight + diagonal:
        copy.wait()

    row = lax.broadcasted_iota(jnp.int32, (ext, lanes), 0)
    lane = lax.broadcasted_iota(jnp.int32, (ext, lanes), 1)
    slot = lane % slots
    group = lane // slots
    rank = group.astype(jnp.float32)
    western = slot < 4
    first_lane = lane == 0
    last_lane = lane == lanes - 1
    beyond = ((row >= h) & (row < h + 4) & (my == ny - 1)) | ((row >= h + 4) & (my == 0))

    def split(from_north, from_south):
        a = jnp.where(half, from_north, from_south)
        b = turn(jnp.where(half, from_south, from_north))
        return a, b

    def tall(main, halo):
        return jnp.concatenate([main, halo], axis=0)

    for k in range(levels):
        d, u = split(y_recv[NORTH, k], y_recv[SOUTH, k])
        v, t = split(y_recv[NORTH, levels + k], y_recv[SOUTH, levels + k])
        wide[DIFF, k, h:ext, :] = d
        wide[EASTWARD, k, h:ext, :] = u
        wide[NORTHWARD, k, h:ext, :] = v
        wide[TEMP, k, h:ext, :] = t
    halo = [split(y_recv[NORTH, 2 * levels + i], y_recv[SOUTH, 2 * levels + i]) for i in range(len(extra))]
    n_main, h_main = tall(n_own, halo[0][0]), tall(h_own, halo[0][1])
    f_main, t_own = tall(f_own, halo[1][0]), tall(t_own, halo[1][1])
    d_own, u_own = tall(d_own, halo[2][0]), tall(u_edge, halo[2][1])
    n_edge, h_edge = tall(n_edge, halo[3][0]), tall(h_edge, halo[3][1])

    x1, x2 = [], []
    for i in (LEFT, RIGHT):
        a, b = split(corner_recv[i, NORTH], corner_recv[i, SOUTH])
        x1.append(tall(x_recv[i, 0], a))
        x2.append(tall(x_recv[i, 1], b))
    d_side = jnp.where(western, x1[LEFT], x1[RIGHT])
    v_side = jnp.where(western, x2[LEFT], x2[RIGHT])
    u_side = jnp.where(western, lroll(x1[LEFT], -4), lroll(x1[RIGHT], 4))
    t_side = jnp.where(western, lroll(x2[LEFT], -4), lroll(x2[RIGHT], 4))
    fields = jnp.where((slot < 2) | (slot >= 6), t_side, 0.0)
    fields = jnp.where((slot == 2) | (slot == 3), lroll(t_side, 2 - 3 * slots), fields)
    fields = jnp.where((slot == 4) | (slot == 5), lroll(t_side, -2 - 3 * slots), fields)
    n_side = spread(jnp.where((group == 0) & ~beyond, fields, 0.0))
    h_side = spread(jnp.where(group == 1, fields, 0.0))
    f_far = lroll(fields, -2 * slots - 4)
    n_far, h_far = lroll(n_side, -4), lroll(h_side, -4)
    n_main = jnp.where(beyond, 0.0, n_main)
    n_edge = jnp.where(beyond, 0.0, n_edge)

    def to_east(x, y):
        a, b = lroll(x, -1), lroll(y, -1)
        return jnp.where(last_lane, b, a), jnp.where(last_lane, a, b)

    def to_west(x, y):
        a, b = lroll(x, 1), lroll(y, 1)
        return jnp.where(first_lane, b, a), jnp.where(first_lane, a, b)

    n_pair, h_pair = (n_main, n_far), (h_main, h_far)
    face_pair = [jnp.minimum(a, b) for a, b in zip(n_pair, to_east(*n_pair))]
    mix_pair = [0.5 * (a + b) for a, b in zip(h_pair, to_east(*h_pair))]
    face_e, mix_e = face_pair[0], mix_pair[0]
    face_n = jnp.minimum(n_main, up(n_main))
    mix_n = 0.5 * (h_main + up(h_main))

    third, fourth = slot == 3, slot == 4

    def from_east(x, edge):
        return lroll(jnp.where(fourth, edge, x), -1)

    face_side = jnp.minimum(n_side, from_east(n_side, n_edge))
    face_edge = jnp.minimum(n_edge, lroll(n_side, -1))
    face_up = jnp.minimum(n_side, up(n_side))
    open_side = jnp.where(rank < face_side, u_side, 0.0)
    open_edge = jnp.where(rank < face_edge, u_own, 0.0)
    open_up = jnp.where(rank < face_up, v_side, 0.0)

    def upwind(speed, here, there):
        return jnp.maximum(speed, 0.0) * here + jnp.minimum(speed, 0.0) * there

    def advect_side(c, edge):
        flux = upwind(open_side, c, from_east(c, edge))
        flux_edge = upwind(open_edge, edge, lroll(c, -1))
        return flux, flux_edge, upwind(open_up, c, up(c))

    def finish_side(c, flux, flux_edge, flux_n):
        flux_w = lroll(jnp.where(third, flux_edge, flux), 1)
        adv = jnp.where(rank < n_side, c - (flux - flux_w + flux_n - down(flux_n)), 0.0)
        return adv, jnp.where(third, flux_edge, lroll(flux, 1))

    flux, flux_edge, flux_n = advect_side(d_side, d_own)
    flux = jnp.where(slot == slots - 1, u_side, flux)
    adv_side, faces_d = finish_side(d_side, flux, flux_edge, flux_n)

    coef_e = jnp.where(rank < face_side, 0.5 * (h_side + from_east(h_side, h_edge)), 0.0)
    coef_edge = jnp.where(rank < face_edge, 0.5 * (h_edge + lroll(h_side, -1)), 0.0)
    coef_n = jnp.where(rank < face_up, 0.5 * (h_side + up(h_side)), 0.0)
    adv_next = lroll(adv_side, -1)
    flow_e = coef_e * (jnp.where(third, 0.0, adv_next) - adv_side)
    flow_edge = coef_edge * adv_next
    flow_w = lroll(jnp.where(third, flow_edge, flow_e), 1)
    flow_n = coef_n * (up(adv_side) - adv_side)
    mixed = adv_side + (flow_e - flow_w) + (flow_n - down(flow_n))
    mixed = jnp.where(slot == slots - 1, lroll(flow_edge, 4), jnp.where(slot == 0, lroll(flow_e, -3), mixed))
    total = spread(mixed)

    near_face = jnp.where(last_lane, face_pair[1], face_e)
    above = row == h + 3
    column = jnp.zeros((ext, lanes), jnp.float32)
    taken_e, given_e, passed_n = column, column, column
    for k in range(levels):
        d = wide[DIFF, k]
        speed = jnp.where(k < face_e, wide[EASTWARD, k], 0.0)
        edge = lroll(faces_d, -(slots * k + 4))
        flux_e = jnp.where(last_lane, edge, upwind(speed, d, lroll(d, -1)))
        flux_w = jnp.where(first_lane, edge, lroll(flux_e, 1))
        v = wide[NORTHWARD, k]
        flux_n = jnp.where(above, v, upwind(jnp.where(k < face_n, v, 0.0), d, up(d)))
        adv = jnp.where(k < n_main, d - (flux_e - flux_w + flux_n - down(flux_n)), 0.0)
        advected[k] = adv
        column = column + adv
        taken_e = taken_e + jnp.where(k < near_face, lroll(adv, -1), 0.0)
        given_e = given_e + jnp.where(k < face_e, adv, 0.0)
        passed_n = passed_n + jnp.where(k < face_n, up(adv) - adv, 0.0)
    at_edge = mix_pair[1] * taken_e
    given_e = mix_e * given_e
    flow_e = jnp.where(last_lane, total, mix_e * taken_e) - given_e
    flow_w = lroll(jnp.where(last_lane, at_edge, flow_e), 1) + jnp.where(first_lane, total, 0.0)
    flow_n = mix_n * passed_n
    rhs_main = f_main + (column + (flow_e - flow_w) + (flow_n - down(flow_n))) / levels
    rhs_far = lroll(total, -4) + jnp.where(last_lane, at_edge, jnp.where(first_lane, lroll(given_e, 1), 0.0))
    rhs_far = f_far + rhs_far / levels

    scale = 1.0 / (levels * SCALE)
    deep = [scale * x for x in n_pair]
    deep_e = [scale * x for x in face_pair]
    deep_w = to_west(*deep_e)
    deep_n = [jnp.minimum(a, up(a)) for a in deep]
    deep_s = [down(a) for a in deep_n]
    base = (0.1 - SHIFT) / SCALE
    centre = [base + ((a + b) + (c + d)) for a, b, c, d in zip(deep_e, deep_w, deep_n, deep_s)]

    def apply(field):
        at_e, at_w = to_east(*field), to_west(*field)
        return tuple(
            centre[i] * field[i] - deep_e[i] * at_e[i] - deep_w[i] * at_w[i]
            - deep_n[i] * up(field[i]) - deep_s[i] * down(field[i])
            for i in range(2)
        )

    v0 = (rhs_main, rhs_far)
    v1 = apply(v0)
    v2 = apply(v1)
    basis = [x[0][:h] for x in (v0, v1, v2)]
    step_e = v2[0] - to_east(*v2)[0]
    step_n = v2[0] - up(v2[0])
    energy = base * (v2[0] * v2[0]) + deep_e[0] * (step_e * step_e) + deep_n[0] * (step_n * step_n)
    products = [basis[m // 2] * basis[m - m // 2] for m in range(2 * ITERS - 1)] + [energy[:h]]
    rows = [jnp.sum(x, axis=0, keepdims=True) for x in products]
    rows.append(jnp.zeros((8 - len(rows), lanes), jnp.float32))
    part = jnp.concatenate(rows, axis=0)
    place = lax.broadcasted_iota(jnp.int32, (8, lanes), 1)
    part = jnp.sum(part, axis=1, keepdims=True)
    part = jnp.where(place == lax.broadcasted_iota(jnp.int32, (8, lanes), 0), part, 0.0)
    part = jnp.sum(part, axis=0, keepdims=True)

    def tracer_stage():
        flux, flux_edge, flux_n = advect_side(t_side, t_own)
        adv_t, faces_t = finish_side(t_side, flux, flux_edge, flux_n)
        swapped = [jnp.where(third, lroll(x, -1), lroll(x, 1)) for x in (adv_t, adv_side)]
        face_w = to_west(*face_pair)[0][:h]
        mix_w = to_west(*mix_pair)[0][:h]
        mix_s = down(mix_n)[:h]
        face_s = down(face_n)[:h]
        last, first = last_lane[:h], first_lane[:h]
        previous_link = zero
        previous = [zero, zero]
        for k in range(levels):
            t = wide[TEMP, k]
            speed = jnp.where(k < face_e, wide[EASTWARD, k], 0.0)
            edge = lroll(faces_t, -(slots * k + 4))
            flux_e = jnp.where(last_lane, edge, upwind(speed, t, lroll(t, -1)))
            flux_w = jnp.where(first_lane, edge, lroll(flux_e, 1))
            flux_n = upwind(jnp.where(k < face_n, wide[NORTHWARD, k], 0.0), t, up(t))
            adv_main = jnp.where(k < n_main, t - (flux_e - flux_w + flux_n - down(flux_n)), 0.0)
            ce = jnp.where(k < face_e[:h], mix_e[:h], 0.0)
            cw = jnp.where(k < face_w, mix_w, 0.0)
            cn = jnp.where(k < face_n[:h], mix_n[:h], 0.0)
            cs = jnp.where(k < face_s, mix_s, 0.0)
            keep = 1.0 - ((ce + cw) + (cn + cs))
            for i, adv in enumerate((adv_main, advected[k])):
                mid = adv[:h]
                edge = lroll(swapped[i][:h], -(slots * k + 4))
                at_e = jnp.where(last, edge, lroll(mid, -1))
                at_w = jnp.where(first, edge, lroll(mid, 1))
                mixed = keep * mid + ce * at_e + cw * at_w + cn * up(adv)[:h] + cs * down(adv)[:h]
                previous[i] = (mixed + previous_link * previous[i]) * inverses[k]
                values[i, k] = previous[i]
            previous_link = jnp.where(k + 1.0 < n_own, coef, 0.0)
        result = previous
        for k in range(levels - 1, -1, -1):
            if k + 1 < levels:
                result = [values[i, k] + ratios[k] * result[i] for i in range(2)]
            rounded[0, k] = result[0].astype(jnp.bfloat16)
            rounded[1, k] = (result[0] + result[1]).astype(jnp.bfloat16)

    if direct:
        parts[me] = part
        pl.semaphore_wait(ready.at[1], len(far))
        copies = []
        for dy in range(ny):
            for dx in range(nx):
                if dx or dy:
                    y, x = lax.rem(my + dy, ny), lax.rem(mx + dx, nx)
                    copies.append(remote(parts.at[me], parts.at[me], send_r, recv_r, dy * nx + dx, y, x))
        for copy in copies:
            copy.start()
        tracer_stage()
        for copy in copies:
            copy.wait()
        total = add_up([parts[i] for i in range(nx * ny)])
    else:
        parts[mx] = part
        copies = []
        for d in range(1, nx):
            copies.append(remote(parts.at[mx], parts.at[mx], send_r, recv_r, d, my, lax.rem(mx + d, nx)))
        for copy in copies:
            copy.start()
        for copy in copies:
            copy.wait()
        mine = nx + my
        parts[mine] = add_up([parts[i] for i in range(nx)])
        copies = []
        for d in range(1, ny):
            copies.append(remote(parts.at[mine], parts.at[mine], send_r, recv_r, nx + d, lax.rem(my + d, ny), mx))
        for copy in copies:
            copy.start()
        tracer_stage()
        for copy in copies:
            copy.wait()
        total = add_up([parts[nx + i] for i in range(ny)])
    moments = [
        jnp.sum(jnp.where(place[:1] == m, total, 0.0), axis=1, keepdims=True) for m in range(2 * ITERS)
    ]
    weights = cg_coefficients(moments)
    out_height[...] = sum(w * b for w, b in zip(weights, basis))


def write_out(rounded, height, out_tracers, out_height, sem):
    copies = [
        pltpu.make_async_copy(rounded, out_tracers, sem.at[0]),
        pltpu.make_async_copy(height, out_height, sem.at[1]),
    ]
    for copy in copies:
        copy.start()
    for copy in copies:
        copy.wait()


def local(tracers, velocities, level_counts, lateral_diffusivity, vertical_diffusivity, forcing):
    levels = tracers.shape[1]
    h, lanes = forcing.shape
    assert tracers.shape[0] == 2 and 8 * levels == lanes and h % 8 == 0
    nx, ny = lax.axis_size("xb"), lax.axis_size("yb")
    assert nx > 2 and ny > 2
    f32 = jnp.float32
    ext = h + 8
    slots = nx * ny if nx * ny <= DIRECT else nx + ny
    planes = 2 * levels + 4
    dma = pltpu.SemaphoreType.DMA
    vmem = pltpu.VMEM
    held = pl.pallas_call(
        functools.partial(kernel, nx, ny, levels),
        out_shape=(vmem(tracers.shape, jnp.bfloat16), vmem(forcing.shape, f32)),
        in_specs=[pl.BlockSpec(memory_space=pl.ANY)] * 6,
        out_specs=(pl.BlockSpec(memory_space=vmem),) * 2,
        scratch_shapes=[
            vmem((4, levels, ext, lanes), f32),
            vmem((levels, h, lanes), f32),
            vmem((h, lanes), jnp.int32),
            vmem((h, lanes), f32),
            vmem((h, lanes), f32),
            vmem((h, lanes), f32),
            vmem((2, 2, h, lanes), f32),
            vmem((2, 2, 8, lanes), f32),
            vmem((2, planes, 8, lanes), f32),
            vmem((2, 2, h, lanes), f32),
            vmem((2, 2, 8, lanes), f32),
            vmem((2, planes, 8, lanes), f32),
            vmem((levels, ext, lanes), f32),
            vmem((2, levels, h, lanes), f32),
            vmem((levels, h, lanes), f32),
            vmem((levels, h, lanes), f32),
            vmem((slots, 1, lanes), f32),
            dma((7,)),
            dma((8,)), dma((8,)),
            dma((slots,)), dma((slots,)),
            pltpu.SemaphoreType.REGULAR((2,)),
        ],
        compiler_params=pltpu.CompilerParams(collective_id=0, has_side_effects=True),
        name="ocean_step",
    )(tracers, velocities, level_counts, lateral_diffusivity, vertical_diffusivity, forcing)
    return pl.pallas_call(
        write_out,
        out_shape=(
            jax.ShapeDtypeStruct(tracers.shape, jnp.bfloat16),
            jax.ShapeDtypeStruct(forcing.shape, f32),
        ),
        in_specs=[pl.BlockSpec(memory_space=vmem)] * 2,
        out_specs=(pl.BlockSpec(memory_space=pl.ANY),) * 2,
        scratch_shapes=[dma((2,))],
        name="write_out",
    )(*[pltpu.with_memory_space_constraint(x, vmem) for x in held])


def solution(mesh):
    return jax.shard_map(
        local,
        mesh=mesh,
        in_specs=(
            P(None, None, "yb", "xb"),
            P(None, None, "yb", "xb"),
            P("yb", "xb"),
            P("yb", "xb"),
            P("yb", "xb"),
            P("yb", "xb"),
        ),
        out_specs=(P(None, None, "yb", "xb"), P("yb", "xb")),
        check_vma=False,
    )
```

time: 24 us -> 19.1 us (0.80)
  Pallas kernels: 23.2 us -> 18.3 us
    pallas_call x1, Pallas kernels: 22.5 us -> 17.6 us  [local(): pl.pallas_call(functools.partial(kernel, nx, ny, levels), out_shape=(vmem...]
where the time goes in v1:
time: 19.1 us; the launch traced here: 18.9 us
  Pallas kernels  18.3 us (96%)
  between operations  0.64 us (3%)
    pallas_call x1, Pallas kernels, local(): pl.pallas_call(functools.partial(kernel, nx, ny, levels), out_shape=(vmem...  17.6 us
    pallas_call x1, Pallas kernels, local(): pl.pallas_call(write_out, out_shape=(jax.ShapeDtypeStruct(tracers.shape,...  0.7 us

profile of v1, /device:TPU:0, one launch (start us, length us, event | category | flops | bytes accessed | tf_op | source)
XLA Modules:
  0.0 18.9 jit_solution(7312488704332236980)
XLA Ops:
  0.6 17.6 %ocean_step.1 = (bf16[2,16,24,128]{3,2,1,0:T(8,128)(2,1)S(1)}, f32[24,128]{1,0:T(8,128)S(1)}) custom-call(f32[2,16,24,128]{3,2,1,0:T(8,128)} %trac.1, f32[2,16,24,128]{3,2,1,0:T(8,128)} %vel.1, s32[24,128]{1,0:T(8,128)} %counts_in.1, f32[24,128]{1,0:T(8,128)} %lateral_in.1, f32[24,128]{1,0:T(8,128)} %vertical_in.1, f32[24,128]{1,0:T(8,128)} %forcing_in.1), custom_call_target="tpu_custom_call" | custom-call | tf_op jit(solution)/shard_map/ocean_step/pallas_call | solution.py:490
  18.2 0.7 %write_out.1 = (bf16[2,16,24,128]{3,2,1,0:T(8,128)(2,1)}, f32[24,128]{1,0:T(8,128)}) custom-call(bf16[2,16,24,128]{3,2,1,0:T(8,128)(2,1)S(1)} %get-tuple-element.4.rounded, f32[24,128]{1,0:T(8,128)S(1)} %get-tuple-element.5.height), custom_call_target="tpu_custom_call" | custom-call | tf_op jit(solution)/shard_map/write_out/pallas_call | solution.py:521

commit v2 on v1

--- a/solution.py
+++ b/solution.py
@@ -57,13 +57,14 @@
     trac, vel, counts_in, lateral_in, vertical_in, forcing_in,
     rounded, out_height,
     wide, salt, counts_i, lateral, kv, force,
-    strips, corners, y_send, x_recv, corner_recv, y_recv,
+    strips, corners, y_send, late_send, x_recv, corner_recv, y_recv, late_recv,
     advected, values, ratios, inverses, parts,
     load_sem, send1, recv1, send_r, recv_r, ready,
 ):
     h, lanes = force.shape
     ext = h + 8
     slots = lanes // levels
+    mid_level = levels // 2
     mx, my = lax.axis_index("xb"), lax.axis_index("yb")
     east, west = lax.rem(mx + 1, nx), lax.rem(mx + nx - 1, nx)
     north, south = lax.rem(my + 1, ny), lax.rem(my + ny - 1, ny)
@@ -89,6 +90,15 @@
         load.start()
     for y, x in peers:
         pl.semaphore_signal(barrier, inc=1, device_id={"xb": x, "yb": y}, device_id_type=MESH)
+
+    def clear(side):
+        y_recv[side] = jnp.zeros(y_recv.shape[1:], jnp.float32)
+        late_recv[side] = jnp.zeros(late_recv.shape[1:], jnp.float32)
+        for i in (LEFT, RIGHT):
+            corner_recv[i, side] = jnp.zeros(corner_recv.shape[2:], jnp.float32)
+
+    pl.when(my == ny - 1)(lambda: clear(NORTH))
+    pl.when(my == 0)(lambda: clear(SOUTH))
     for load in loads:
         load.wait()
 
@@ -130,6 +140,7 @@
         return jnp.where(half, turn(b[h - 8:]), a[h - 8:])
 
     pack = [jnp.zeros((h, lanes), jnp.float32)] * 4
+    lows = []
     for k in range(levels):
         t = wide[TEMP, k, 0:h, :]
         u = wide[EASTWARD, k, 0:h, :]
@@ -144,9 +155,14 @@
         flux = jnp.maximum(v[:8], 0.0) * d[:8] + jnp.minimum(v[:8], 0.0) * up(d[:8])
         v_low = jnp.where(fourth, jnp.where(k < face_low, flux, 0.0), v[:8])
         y_send[NORTH, k] = low_pair(d, u)
-        y_send[NORTH, levels + k] = low_pair(v_low, t)
+        lows.append(v_low)
         y_send[SOUTH, k] = high_pair(d, u)
-        y_send[SOUTH, levels + k] = high_pair(v, t)
+        if k >= mid_level:
+            i = k - mid_level
+            y_send[NORTH, levels + i] = low_pair(lows[i], v_low)
+            y_send[SOUTH, levels + i] = high_pair(wide[NORTHWARD, i, 0:h, :], v)
+            late_send[NORTH, i] = low_pair(wide[TEMP, i, 0:h, :], t)
+            late_send[SOUTH, i] = high_pair(wide[TEMP, i, 0:h, :], t)
     t_own, d_own, u_edge, v_edge = pack
     for i, x in enumerate((n_own, h_own, f_own)):
         a, b = slots * i, slots * (i + 3)
@@ -167,8 +183,8 @@
         corners[i, SOUTH] = high_pair(a, b)
     extra = [(n_own, h_own), (f_own, t_own), (d_own, u_edge), (n_edge, h_edge)]
     for i, (a, b) in enumerate(extra):
-        y_send[NORTH, 2 * levels + i] = low_pair(a, b)
-        y_send[SOUTH, 2 * levels + i] = high_pair(a, b)
+        y_send[NORTH, levels + mid_level + i] = low_pair(a, b)
+        y_send[SOUTH, levels + mid_level + i] = high_pair(a, b)
 
     pl.semaphore_wait(barrier, len(peers))
 
@@ -180,26 +196,64 @@
 
     for y, x in near:
         pl.semaphore_signal(ready.at[0], inc=1, device_id={"xb": x, "yb": y}, device_id_type=MESH)
-    straight = [
-        remote(strips.at[0], x_recv.at[LEFT], send1, recv1, 4, my, east),
-        remote(strips.at[1], x_recv.at[RIGHT], send1, recv1, 5, my, west),
-        remote(y_send.at[SOUTH], y_recv.at[SOUTH], send1, recv1, 6, north, mx),
-        remote(y_send.at[NORTH], y_recv.at[NORTH], send1, recv1, 7, south, mx),
-    ]
-    diagonal = [
-        remote(corners.at[0, SOUTH], corner_recv.at[LEFT, SOUTH], send1, recv1, 0, north, east),
-        remote(corners.at[0, NORTH], corner_recv.at[LEFT, NORTH], send1, recv1, 1, south, east),
-        remote(corners.at[1, SOUTH], corner_recv.at[RIGHT, SOUTH], send1, recv1, 2, north, west),
-        remote(corners.at[1, NORTH], corner_recv.at[RIGHT, NORTH], send1, recv1, 3, south, west),
-    ]
-    for copy in straight:
+    strip_copies = [
+        remote(strips.at[0], x_recv.at[LEFT], send1, recv1, 0, my, east),
+        remote(strips.at[1], x_recv.at[RIGHT], send1, recv1, 1, my, west),
+    ]
+    row_copies = [
+        [remote(y_send.at[SOUTH], y_recv.at[SOUTH], send1, recv1, 2, north, mx)],
+        [remote(y_send.at[NORTH], y_recv.at[NORTH], send1, recv1, 3, south, mx)],
+    ]
+    corner_copies = [
+        [
+            remote(corners.at[0, SOUTH], corner_recv.at[LEFT, SOUTH], send1, recv1, 4, north, east),
+            remote(corners.at[1, SOUTH], corner_recv.at[RIGHT, SOUTH], send1, recv1, 5, north, west),
+        ],
+        [
+            remote(corners.at[0, NORTH], corner_recv.at[LEFT, NORTH], send1, recv1, 6, south, east),
+            remote(corners.at[1, NORTH], corner_recv.at[RIGHT, NORTH], send1, recv1, 7, south, west),
+        ],
+    ]
+    late_copies = [
+        [remote(late_send.at[SOUTH], late_recv.at[SOUTH], send1, recv1, 8, north, mx)],
+        [remote(late_send.at[NORTH], late_recv.at[NORTH], send1, recv1, 9, south, mx)],
+    ]
+
+    def begin(northward, southward):
+        @pl.when(my < ny - 1)
+        def _():
+            for copy in northward:
+                copy.start()
+
+        @pl.when(my > 0)
+        def _():
+            for copy in southward:
+                copy.start()
+
+    def finish(northward, southward):
+        @pl.when(my < ny - 1)
+        def _():
+            for copy in northward:
+                copy.wait_send()
+            for copy in southward:
+                copy.wait_recv()
+
+        @pl.when(my > 0)
+        def _():
+            for copy in northward:
+                copy.wait_recv()
+            for copy in southward:
+                copy.wait_send()
+
+    begin(*row_copies)
+    for copy in strip_copies:
         copy.start()
     if direct:
         for y, x in far:
             pl.semaphore_signal(ready.at[1], inc=1, device_id={"xb": x, "yb": y}, device_id_type=MESH)
     pl.semaphore_wait(ready.at[0], len(near))
-    for copy in diagonal:
-        copy.start()
+    begin(*corner_copies)
+    begin(*late_copies)
 
     coef = kv[...]
     zero = jnp.zeros_like(coef)
@@ -213,8 +267,7 @@
         inverses[k] = inverse
         ratios[k] = previous_ratio
 
-    for copy in straight + diagonal:
-        copy.wait()
+    finish(*row_copies)
 
     row = lax.broadcasted_iota(jnp.int32, (ext, lanes), 0)
     lane = lax.broadcasted_iota(jnp.int32, (ext, lanes), 1)
@@ -236,16 +289,54 @@
 
     for k in range(levels):
         d, u = split(y_recv[NORTH, k], y_recv[SOUTH, k])
-        v, t = split(y_recv[NORTH, levels + k], y_recv[SOUTH, levels + k])
         wide[DIFF, k, h:ext, :] = d
         wide[EASTWARD, k, h:ext, :] = u
-        wide[NORTHWARD, k, h:ext, :] = v
-        wide[TEMP, k, h:ext, :] = t
-    halo = [split(y_recv[NORTH, 2 * levels + i], y_recv[SOUTH, 2 * levels + i]) for i in range(len(extra))]
+    for k in range(mid_level):
+        a, b = split(y_recv[NORTH, levels + k], y_recv[SOUTH, levels + k])
+        wide[NORTHWARD, k, h:ext, :] = a
+        wide[NORTHWARD, mid_level + k, h:ext, :] = b
+    first = levels + mid_level
+    halo = [split(y_recv[NORTH, first + i], y_recv[SOUTH, first + i]) for i in range(len(extra))]
     n_main, h_main = tall(n_own, halo[0][0]), tall(h_own, halo[0][1])
     f_main, t_own = tall(f_own, halo[1][0]), tall(t_own, halo[1][1])
     d_own, u_own = tall(d_own, halo[2][0]), tall(u_edge, halo[2][1])
     n_edge, h_edge = tall(n_edge, halo[3][0]), tall(h_edge, halo[3][1])
+
+    n_main = jnp.where(beyond, 0.0, n_main)
+    n_edge = jnp.where(beyond, 0.0, n_edge)
+
+    def upwind(speed, here, there):
+        return jnp.maximum(speed, 0.0) * here + jnp.minimum(speed, 0.0) * there
+
+    inner_e = jnp.where(last_lane, 0.0, jnp.minimum(n_main, lroll(n_main, -1)))
+    inner_mix = 0.5 * (h_main + lroll(h_main, -1))
+    face_n = jnp.minimum(n_main, up(n_main))
+    mix_n = 0.5 * (h_main + up(h_main))
+    above = row == h + 3
+    column = jnp.zeros((ext, lanes), jnp.float32)
+    passed_e, passed_n, a_own = column, column, column
+    for k in range(levels):
+        d = wide[DIFF, k]
+        flux_e = upwind(jnp.where(k < inner_e, wide[EASTWARD, k], 0.0), d, lroll(d, -1))
+        v = wide[NORTHWARD, k]
+        flux_n = jnp.where(above, v, upwind(jnp.where(k < face_n, v, 0.0), d, up(d)))
+        adv = jnp.where(k < n_main, d - (flux_e - lroll(flux_e, 1) + flux_n - down(flux_n)), 0.0)
+        advected[k] = adv
+        column = column + adv
+        passed_e = passed_e + jnp.where(k < inner_e, lroll(adv, -1) - adv, 0.0)
+        passed_n = passed_n + jnp.where(k < face_n, up(adv) - adv, 0.0)
+        a_own = jnp.where(group == k, lroll(adv, slots * k + 4), a_own)
+    flow_e = inner_mix * passed_e
+    flow_n = mix_n * passed_n
+    mixed_main = column + (flow_e - lroll(flow_e, 1)) + (flow_n - down(flow_n))
+
+    third, fourth = slot == 3, slot == 4
+    coef_own = jnp.where(rank < jnp.minimum(n_edge, lroll(n_edge, -1)), 0.5 * (h_edge + lroll(h_edge, -1)), 0.0)
+    coef_own_n = jnp.where(rank < jnp.minimum(n_edge, up(n_edge)), 0.5 * (h_edge + up(h_edge)), 0.0)
+
+    for copy in strip_copies:
+        copy.wait()
+    finish(*corner_copies)
 
     x1, x2 = [], []
     for i in (LEFT, RIGHT):
@@ -263,8 +354,6 @@
     h_side = spread(jnp.where(group == 1, fields, 0.0))
     f_far = lroll(fields, -2 * slots - 4)
     n_far, h_far = lroll(n_side, -4), lroll(h_side, -4)
-    n_main = jnp.where(beyond, 0.0, n_main)
-    n_edge = jnp.where(beyond, 0.0, n_edge)
 
     def to_east(x, y):
         a, b = lroll(x, -1), lroll(y, -1)
@@ -276,12 +365,6 @@
 
     n_pair, h_pair = (n_main, n_far), (h_main, h_far)
     face_pair = [jnp.minimum(a, b) for a, b in zip(n_pair, to_east(*n_pair))]
-    mix_pair = [0.5 * (a + b) for a, b in zip(h_pair, to_east(*h_pair))]
-    face_e, mix_e = face_pair[0], mix_pair[0]
-    face_n = jnp.minimum(n_main, up(n_main))
-    mix_n = 0.5 * (h_main + up(h_main))
-
-    third, fourth = slot == 3, slot == 4
 
     def from_east(x, edge):
         return lroll(jnp.where(fourth, edge, x), -1)
@@ -293,9 +376,6 @@
     open_edge = jnp.where(rank < face_edge, u_own, 0.0)
     open_up = jnp.where(rank < face_up, v_side, 0.0)
 
-    def upwind(speed, here, there):
-        return jnp.maximum(speed, 0.0) * here + jnp.minimum(speed, 0.0) * there
-
     def advect_side(c, edge):
         flux = upwind(open_side, c, from_east(c, edge))
         flux_edge = upwind(open_edge, edge, lroll(c, -1))
@@ -304,7 +384,7 @@
     def finish_side(c, flux, flux_edge, flux_n):
         flux_w = lroll(jnp.where(third, flux_edge, flux), 1)
         adv = jnp.where(rank < n_side, c - (flux - flux_w + flux_n - down(flux_n)), 0.0)
-        return adv, jnp.where(third, flux_edge, lroll(flux, 1))
+        return adv, jnp.where(third, flux_edge, jnp.where(fourth, lroll(flux, 1), 0.0))
 
     flux, flux_edge, flux_n = advect_side(d_side, d_own)
     flux = jnp.where(slot == slots - 1, u_side, flux)
@@ -313,40 +393,20 @@
     coef_e = jnp.where(rank < face_side, 0.5 * (h_side + from_east(h_side, h_edge)), 0.0)
     coef_edge = jnp.where(rank < face_edge, 0.5 * (h_edge + lroll(h_side, -1)), 0.0)
     coef_n = jnp.where(rank < face_up, 0.5 * (h_side + up(h_side)), 0.0)
-    adv_next = lroll(adv_side, -1)
-    flow_e = coef_e * (jnp.where(third, 0.0, adv_next) - adv_side)
-    flow_edge = coef_edge * adv_next
+    gained = jnp.where(rank < n_edge, jnp.where(third, -faces_d, faces_d), 0.0)
+    a_own = a_own + gained
+    flow_e = coef_e * (from_east(adv_side, a_own) - adv_side)
+    flow_edge = coef_edge * (lroll(adv_side, -1) - a_own)
     flow_w = lroll(jnp.where(third, flow_edge, flow_e), 1)
     flow_n = coef_n * (up(adv_side) - adv_side)
     mixed = adv_side + (flow_e - flow_w) + (flow_n - down(flow_n))
-    mixed = jnp.where(slot == slots - 1, lroll(flow_edge, 4), jnp.where(slot == 0, lroll(flow_e, -3), mixed))
-    total = spread(mixed)
-
-    near_face = jnp.where(last_lane, face_pair[1], face_e)
-    above = row == h + 3
-    column = jnp.zeros((ext, lanes), jnp.float32)
-    taken_e, given_e, passed_n = column, column, column
-    for k in range(levels):
-        d = wide[DIFF, k]
-        speed = jnp.where(k < face_e, wide[EASTWARD, k], 0.0)
-        edge = lroll(faces_d, -(slots * k + 4))
-        flux_e = jnp.where(last_lane, edge, upwind(speed, d, lroll(d, -1)))
-        flux_w = jnp.where(first_lane, edge, lroll(flux_e, 1))
-        v = wide[NORTHWARD, k]
-        flux_n = jnp.where(above, v, upwind(jnp.where(k < face_n, v, 0.0), d, up(d)))
-        adv = jnp.where(k < n_main, d - (flux_e - flux_w + flux_n - down(flux_n)), 0.0)
-        advected[k] = adv
-        column = column + adv
-        taken_e = taken_e + jnp.where(k < near_face, lroll(adv, -1), 0.0)
-        given_e = given_e + jnp.where(k < face_e, adv, 0.0)
-        passed_n = passed_n + jnp.where(k < face_n, up(adv) - adv, 0.0)
-    at_edge = mix_pair[1] * taken_e
-    given_e = mix_e * given_e
-    flow_e = jnp.where(last_lane, total, mix_e * taken_e) - given_e
-    flow_w = lroll(jnp.where(last_lane, at_edge, flow_e), 1) + jnp.where(first_lane, total, 0.0)
-    flow_n = mix_n * passed_n
-    rhs_main = f_main + (column + (flow_e - flow_w) + (flow_n - down(flow_n))) / levels
-    rhs_far = lroll(total, -4) + jnp.where(last_lane, at_edge, jnp.where(first_lane, lroll(given_e, 1), 0.0))
+    inner = coef_own * jnp.where(slot == 2, lroll(gained, -1), jnp.where(fourth, -gained, 0.0))
+    flow_w = lroll(jnp.where(third, flow_e, inner), 1)
+    flow_n = coef_own_n * (up(gained) - gained)
+    mixed_own = gained + (jnp.where(third, flow_edge, inner) - flow_w) + (flow_n - down(flow_n))
+    rhs_far = lroll(spread(mixed), -4)
+    added = lroll(spread(mixed_own), -4)
+    rhs_main = f_main + (mixed_main + jnp.where((lane >= lanes - 2) | (lane < 2), added, 0.0)) / levels
     rhs_far = f_far + rhs_far / levels
 
     scale = 1.0 / (levels * SCALE)
@@ -383,8 +443,16 @@
     part = jnp.sum(part, axis=0, keepdims=True)
 
     def tracer_stage():
+        finish(*late_copies)
+        for k in range(mid_level):
+            a, b = split(late_recv[NORTH, k], late_recv[SOUTH, k])
+            wide[TEMP, k, h:ext, :] = a
+            wide[TEMP, mid_level + k, h:ext, :] = b
         flux, flux_edge, flux_n = advect_side(t_side, t_own)
         adv_t, faces_t = finish_side(t_side, flux, flux_edge, flux_n)
+        mix_pair = [0.5 * (a + b) for a, b in zip(h_pair, to_east(*h_pair))]
+        face_e, mix_e = face_pair[0], mix_pair[0]
+        rim = first_lane | last_lane
         swapped = [jnp.where(third, lroll(x, -1), lroll(x, 1)) for x in (adv_t, adv_side)]
         face_w = to_west(*face_pair)[0][:h]
         mix_w = to_west(*mix_pair)[0][:h]
@@ -406,7 +474,8 @@
             cn = jnp.where(k < face_n[:h], mix_n[:h], 0.0)
             cs = jnp.where(k < face_s, mix_s, 0.0)
             keep = 1.0 - ((ce + cw) + (cn + cs))
-            for i, adv in enumerate((adv_main, advected[k])):
+            adv_d = jnp.where(rim, lroll(a_own, -(slots * k + 4)), advected[k])
+            for i, adv in enumerate((adv_main, adv_d)):
                 mid = adv[:h]
                 edge = lroll(swapped[i][:h], -(slots * k + 4))
                 at_e = jnp.where(last, edge, lroll(mid, -1))
@@ -484,7 +553,7 @@
     f32 = jnp.float32
     ext = h + 8
     slots = nx * ny if nx * ny <= DIRECT else nx + ny
-    planes = 2 * levels + 4
+    planes = levels + levels // 2 + 4
     dma = pltpu.SemaphoreType.DMA
     vmem = pltpu.VMEM
     held = pl.pallas_call(
@@ -502,16 +571,18 @@
             vmem((2, 2, h, lanes), f32),
             vmem((2, 2, 8, lanes), f32),
             vmem((2, planes, 8, lanes), f32),
+            vmem((2, levels // 2, 8, lanes), f32),
             vmem((2, 2, h, lanes), f32),
             vmem((2, 2, 8, lanes), f32),
             vmem((2, planes, 8, lanes), f32),
+            vmem((2, levels // 2, 8, lanes), f32),
             vmem((levels, ext, lanes), f32),
             vmem((2, levels, h, lanes), f32),
             vmem((levels, h, lanes), f32),
             vmem((levels, h, lanes), f32),
             vmem((slots, 1, lanes), f32),
             dma((7,)),
-            dma((8,)), dma((8,)),
+            dma((10,)), dma((10,)),
             dma((slots,)), dma((slots,)),
             pltpu.SemaphoreType.REGULAR((2,)),
         ],

time: 19.1 us -> 18.9 us (0.990)
  Pallas kernels: 18.3 us -> 18.1 us
where the time goes in v2:
time: 18.9 us; the launch traced here: 18.7 us
  Pallas kernels  18.1 us (96%)
  between operations  0.64 us (3%)
    pallas_call x1, Pallas kernels, local(): pl.pallas_call(functools.partial(kernel, nx, ny, levels), out_shape=(vmem...  17.4 us
    pallas_call x1, Pallas kernels, local(): pl.pallas_call(write_out, out_shape=(jax.ShapeDtypeStruct(tracers.shape,...  0.7 us

profile of v2, /device:TPU:0, one launch (start us, length us, event | category | flops | bytes accessed | tf_op | source)
XLA Modules:
  0.0 18.7 jit_solution(17034915015617906823)
XLA Ops:
  0.6 17.4 %ocean_step.1 = (bf16[2,16,24,128]{3,2,1,0:T(8,128)(2,1)S(1)}, f32[24,128]{1,0:T(8,128)S(1)}) custom-call(f32[2,16,24,128]{3,2,1,0:T(8,128)} %trac.1, f32[2,16,24,128]{3,2,1,0:T(8,128)} %vel.1, s32[24,128]{1,0:T(8,128)} %counts_in.1, f32[24,128]{1,0:T(8,128)} %lateral_in.1, f32[24,128]{1,0:T(8,128)} %vertical_in.1, f32[24,128]{1,0:T(8,128)} %forcing_in.1), custom_call_target="tpu_custom_call" | custom-call | tf_op jit(solution)/shard_map/ocean_step/pallas_call | solution.py:559
  18.0 0.7 %write_out.1 = (bf16[2,16,24,128]{3,2,1,0:T(8,128)(2,1)}, f32[24,128]{1,0:T(8,128)}) custom-call(bf16[2,16,24,128]{3,2,1,0:T(8,128)(2,1)S(1)} %get-tuple-element.4.rounded, f32[24,128]{1,0:T(8,128)S(1)} %get-tuple-element.5.height), custom_call_target="tpu_custom_call" | custom-call | tf_op jit(solution)/shard_map/write_out/pallas_call | solution.py:592

commit v3 on v2

--- a/solution.py
+++ b/solution.py
@@ -499,12 +499,12 @@
             for dx in range(nx):
                 if dx or dy:
                     y, x = lax.rem(my + dy, ny), lax.rem(mx + dx, nx)
-                    copies.append(remote(parts.at[me], parts.at[me], send_r, recv_r, dy * nx + dx, y, x))
+                    copies.append(remote(parts.at[me], parts.at[me], send_r, recv_r, 0, y, x))
         for copy in copies:
             copy.start()
         tracer_stage()
-        for copy in copies:
-            copy.wait()
+        others = pl.ds(0, nx * ny - 1)
+        remote(parts.at[others], parts.at[others], send_r, recv_r, 0, north, mx).wait()
         total = add_up([parts[i] for i in range(nx * ny)])
     else:
         parts[mx] = part

time: 18.9 us -> 18.8 us (level)
  no operation moved by 1% of the time
where the time goes in v3:
time: 18.8 us; the launch traced here: 18.7 us
  Pallas kernels  18 us (96%)
  between operations  0.64 us (3%)
    pallas_call x1, Pallas kernels, local(): pl.pallas_call(functools.partial(kernel, nx, ny, levels), out_shape=(vmem...  17.3 us
    pallas_call x1, Pallas kernels, local(): pl.pallas_call(write_out, out_shape=(jax.ShapeDtypeStruct(tracers.shape,...  0.7 us

profile of v3, /device:TPU:0, one launch (start us, length us, event | category | flops | bytes accessed | tf_op | source)
XLA Modules:
  0.0 18.7 jit_solution(10573506060364649348)
XLA Ops:
  0.6 17.3 %ocean_step.1 = (bf16[2,16,24,128]{3,2,1,0:T(8,128)(2,1)S(1)}, f32[24,128]{1,0:T(8,128)S(1)}) custom-call(f32[2,16,24,128]{3,2,1,0:T(8,128)} %trac.1, f32[2,16,24,128]{3,2,1,0:T(8,128)} %vel.1, s32[24,128]{1,0:T(8,128)} %counts_in.1, f32[24,128]{1,0:T(8,128)} %lateral_in.1, f32[24,128]{1,0:T(8,128)} %vertical_in.1, f32[24,128]{1,0:T(8,128)} %forcing_in.1), custom_call_target="tpu_custom_call" | custom-call | tf_op jit(solution)/shard_map/ocean_step/pallas_call | solution.py:559
  18.0 0.7 %write_out.1 = (bf16[2,16,24,128]{3,2,1,0:T(8,128)(2,1)}, f32[24,128]{1,0:T(8,128)}) custom-call(bf16[2,16,24,128]{3,2,1,0:T(8,128)(2,1)S(1)} %get-tuple-element.4.rounded, f32[24,128]{1,0:T(8,128)S(1)} %get-tuple-element.5.height), custom_call_target="tpu_custom_call" | custom-call | tf_op jit(solution)/shard_map/write_out/pallas_call | solution.py:592
